TPU v7x, 32 devices: a whole 2x2x4 slice. The times are simulated.
32 devices in a mesh: grp: 2 (over x), tpl: 16 (over z, y, core).
Axes of the slice: x: 2, y: 2, z: 4, core: 2. Of those that a mesh axis runs over, the one named last changes fastest.
Arguments:
- strain_slots: bfloat16 [32, 3, 2, 262144], P(('grp', 'tpl')), parts along dimension 0, may hold values from -6 to 6
- templates: bfloat16 [32, 2, 262144], P(None, None, 'tpl'), may hold values from -6 to 6
- cutoffs: int32 [32], replicated, may hold values from 32768 to 262144
- lists: int32 [16, 2], replicated, may hold values from 0 to 31, as said below
- owner: int32 [2], P('grp'), parts along dimension 0, may hold values from 0 to 15
- slides: int32 [6], P('grp'), parts along dimension 0, may hold values from 0 to 262143
Outputs:
- peaks: float32 [64], P(('grp', 'tpl')), parts along dimension 0
- norms: float32 [64], P(('grp', 'tpl')), parts along dimension 0
There are 2 independent parts, one for each index of `grp`. A program takes and returns all parts, laid end to end along the dimension named above; an argument that names none is the same for every part. Nothing has to cross between parts.
Inputs may be any that keep to these rules, and one draw needn't show every extreme that they name: Every template appears once in lists; list positions in row-major order run through the templates by falling cutoffs. One template has cutoff 262144, one has 32768.
All inputs are finite; a program needn't handle non-finite values.
Results may differ from a plain program's by a relative error of at most 0.0021.
Values may be sent and summed in bfloat16 or wider, within the bound.
A program may use at most 128 MiB of HBM per device.

v0:
```python
import jax
import jax.numpy as jnp
from jax import lax
from jax.sharding import PartitionSpec as P

DET = 3
ROWS = 512
COLS = 512
BLOCK_ROWS = 64
two_pi = 6.283185307179586
eps_norm = 1e-06


def spread(block, axis, owner):
    block = jnp.where(lax.axis_index(axis) == owner, block, jnp.zeros_like(block))
    return lax.psum(block, axis)


def turn_table(left_ids, right_ids, period):
    product_idx = left_ids[:, None] * right_ids[None, :] % period
    angles = product_idx.astype(jnp.float32) * (two_pi / period)
    return (jnp.cos(angles), jnp.sin(angles))


def slide_phases(slides):
    total = ROWS * COLS
    bin_ids = jnp.arange(total, dtype=jnp.int32)
    row_ids = bin_ids // COLS
    col_ids = bin_ids % COLS
    stride = COLS * slides % total
    turns = (
        row_ids[None, :] * stride[:, None] % total + col_ids[None, :] * slides[:, None] % total
    ) % total
    angles = turns.astype(jnp.float32) * (two_pi / total)
    return (jnp.cos(angles), jnp.sin(angles))


def body(strain_slots, templates, cutoffs, lists, owner, slides):
    total = ROWS * COLS
    block_count_all = ROWS // BLOCK_ROWS
    devices = lax.axis_size("tpl")
    own_index = lax.axis_index("tpl")
    per_device = lists.shape[1]
    strain = spread(strain_slots[0], "tpl", owner[0])
    flat_list = lists.reshape(-1)
    device_ids = jnp.arange(devices, dtype=jnp.int32)[:, None]
    slot_ids = jnp.arange(per_device, dtype=jnp.int32)[None, :]
    positions = device_ids * per_device + slot_ids
    chosen = flat_list[positions]
    picked = templates[chosen.reshape(-1)]
    picked = picked.reshape(devices, per_device, 2, templates.shape[2])
    arrived = lax.all_to_all(picked, "tpl", split_axis=0, concat_axis=3, tiled=True)[0]
    own_ids = lax.dynamic_index_in_dim(chosen, own_index, 0, keepdims=False)
    cutoff_bins = cutoffs[own_ids]
    row_ids = jnp.arange(ROWS, dtype=jnp.int32)
    col_ids = jnp.arange(COLS, dtype=jnp.int32)
    row_cos, row_sin = turn_table(row_ids, row_ids, ROWS)
    cos_blocks = row_cos.reshape(ROWS, block_count_all, BLOCK_ROWS).transpose(1, 0, 2)
    sin_blocks = row_sin.reshape(ROWS, block_count_all, BLOCK_ROWS).transpose(1, 0, 2)
    row_blocks = jnp.concatenate(
        [
            jnp.concatenate([cos_blocks, -sin_blocks], 2),
            jnp.concatenate([sin_blocks, cos_blocks], 2),
        ],
        1,
    ).astype(jnp.bfloat16)
    twiddle_cos, twiddle_sin = turn_table(row_ids, col_ids, total)
    col_cos, col_sin = turn_table(col_ids, col_ids, COLS)
    col_table = jnp.concatenate(
        [jnp.concatenate([col_cos, col_sin], 1), jnp.concatenate([-col_sin, col_cos], 1)], 0
    ).astype(jnp.bfloat16)
    phase_cos, phase_sin = slide_phases(slides)
    data_re = strain[:, 0].astype(jnp.float32)
    data_im = strain[:, 1].astype(jnp.float32)

    def filter_one(packed):
        waveform, cutoff = packed
        inside = jnp.arange(total, dtype=jnp.int32) < cutoff
        wave_re = waveform[0].astype(jnp.float32)
        wave_im = waveform[1].astype(jnp.float32)
        real_part = data_re * wave_re + data_im * wave_im
        imag_part = data_im * wave_re - data_re * wave_im
        prod_re = jnp.where(inside, real_part * phase_cos - imag_part * phase_sin, 0.0)
        prod_im = jnp.where(inside, real_part * phase_sin + imag_part * phase_cos, 0.0)
        stacked = jnp.concatenate(
            [
                prod_re.reshape(DET, block_count_all, BLOCK_ROWS, COLS),
                prod_im.reshape(DET, block_count_all, BLOCK_ROWS, COLS),
            ],
            2,
        ).astype(jnp.bfloat16)
        section_one = jnp.einsum(
            "bai,dbic->dac", row_blocks, stacked, preferred_element_type=jnp.float32
        )
        first_re = section_one[:, :ROWS]
        first_im = section_one[:, ROWS:]
        twisted = jnp.concatenate(
            [
                first_re * twiddle_cos - first_im * twiddle_sin,
                first_re * twiddle_sin + first_im * twiddle_cos,
            ],
            2,
        ).astype(jnp.bfloat16)
        series = jnp.einsum("dab,bc->dac", twisted, col_table, preferred_element_type=jnp.float32)
        squares = jnp.sum(series * series, axis=0)
        power_sum = squares[:, :COLS] + squares[:, COLS:]
        sigmasq = jnp.sum(jnp.where(inside, wave_re * wave_re + wave_im * wave_im, 0.0))
        return (jnp.max(power_sum) / (2.0 * (sigmasq + eps_norm)), sigmasq / total)

    peaks, norms = lax.map(filter_one, (arrived, cutoff_bins))
    return (peaks, norms)


def solution(mesh):
    in_specs = (
        P(("grp", "tpl"), None, None, None),
        P(None, None, "tpl"),
        P(),
        P(),
        P("grp"),
        P("grp"),
    )
    out_specs = (P(("grp", "tpl")), P(("grp", "tpl")))
    return jax.shard_map(body, mesh=mesh, in_specs=in_specs, out_specs=out_specs, check_vma=False)
```

profile of v0, /device:TPU:0, one launch (start us, length us, event | category | flops | bytes accessed | tf_op | source)
XLA Modules:
  0.0 458.4 jit_solution(1903081071991389454)
XLA Ops:
  8.0 10.3 %fusion.41 = bf16[3,2,262144]{2,0,1:T(4,128)(2,1)} fusion(bf16[1,3,2,262144]{3,2,1,0:T(2,128)(2,1)} %param.8, pred[]{:T(512)S(6)} %eq.15), kind=kLoop, calls=%fused_computation.69 | loop fusion | flops 1572864 | bytes 6291457 | tf_op jit(solution)/shard_map/jit(_where)/select_n | solution.py:15
  19.9 6.1 %gather_fusion.2 = bf16[32,2,16384]{2,1,0:T(2,128)(2,1)} fusion(bf16[32,2,16384]{2,1,0:T(2,128)(2,1)S(1)} %copy-done, s32[1024]{0:T(1024)S(1)} %pad_clamp_fusion), kind=kCustom, calls=%fused_computation.2 | custom fusion | bytes 4194432 | tf_op jit(solution)/shard_map/gather | solution.py:50
  26.0 7.8 %all-to-all-start = ((bf16[16,2,2,16384]{3,2,1,0:T(2,128)(2,1)}), bf16[16,2,2,16384]{3,2,1,0:T(2,128)(2,1)}, u32[]{:S(2)}, u32[]{:S(2)}) async-start(bf16[16,2,2,16384]{3,2,1,0:T(2,128)(2,1)} %bitcast.96), calls=%async_computation | async-start | bytes 4194304 | tf_op jit(solution)/shard_map/all_to_all | solution.py:52
  33.8 1.5 fusion.49
  36.1 4.0 fusion.66
  40.1 4.3 negate_convert_fusion.1
  44.4 8.7 %negate_convert_fusion = (bf16[8,512,64]{2,1,0:T(8,128)(2,1)S(1)}, bf16[8,512,64]{2,1,0:T(8,128)(2,1)S(1)}, bf16[8,512,64]{2,1,0:T(8,128)(2,1)S(1)}) fusion(s32[8,64]{1,0:T(8,128)S(1)} %multiply_add_fusion.2), kind=kLoop, calls=%fused_computation.82 | loop fusion | flops 4718592 | bytes 1574912 | tf_op jit(solution)/shard_map/convert.19
  53.1 2.5 maximum_maximum_fusion
  55.6 1.6 maximum_maximum_fusion.1
  57.2 115.2 %all-reduce.2.cloned.1.call-done = bf16[3,2,262144]{2,0,1:T(4,128)(2,1)} async-done(((bf16[3,2,262144]{2,0,1:T(4,128)(2,1)}), bf16[3,2,262144]{2,0,1:T(4,128)(2,1)}) %all-reduce.2.cloned.1.call-update) | async-done | bytes 3145744 | tf_op jit(solution)/shard_map/psum | solution.py:16
  172.4 5.0 %fusion.45 = (f32[3,262144]{1,0:T(4,128)}, f32[3,262144]{1,0:T(4,128)}) fusion(bf16[3,2,262144]{2,0,1:T(4,128)(2,1)} %all-reduce.2.cloned.1.call-done), kind=kLoop, calls=%fused_computation.77 | loop fusion | flops 1572864 | bytes 9437184 | tf_op jit(solution)/shard_map/convert_element_type | solution.py:74
  177.4 2.7 copy.68
  180.1 2.5 squeeze.23
  182.7 267.2 %while.15 = (s32[]{:T(128)}, f32[2]{0:T(128)S(1)}, f32[2]{0:T(128)S(1)}, s32[2]{0:T(128)S(1)}, f32[3,262144]{1,0:T(4,128)}, /*index=5*/bf16[2,2,262144]{2,1,0:T(...) while((s32[]{:T(128)}, f32[2]{0:T(128)S(1)}, ...), condition=%wide.region_5.6_spmd.clone.clone.clone, body=%wide.region_1.5_spmd.clone.clone.clone.sunk | while | flops 6514016256 | bytes 146276784 | solution.py:110
  183.0 16.5 %fusion.84 = (f32[262144]{0:T(1024)}, f32[262144]{0:T(1024)S(1)}, f32[1,1,262144]{2,1,0:T(1,128)}) fusion(bf16[2,2,262144]{2,1,0:T(2,128)(2,1)} %get-tuple-element.387, s32[]{:T(128)} %get-tuple-element.363, s32[]{:T(128)S(6)} %add.959), kind=kLoop, calls=%fused_computation.62.clone.1 | loop fusion | flops 1310720 | bytes 4194312 | tf_op jit(solution)/shard_map/while/body/eval_jaxpr/convert_element_type | solution.py:79
  200.3 1.4 reshape.324
  201.7 1.9 copy.97
  205.2 42.2 %fusion.83 = (f32[3,262144]{1,0:T(4,128)S(1)}, f32[3,262144]{1,0:T(4,128)}) fusion(s32[3]{0:T(128)S(1)} %get-tuple-element.393, s32[262144]{0:T(1024)} %get-tuple-element.394, s32[3]{0:T(128)S(1)} %get-tuple-element.391, s32[262144]{0:T(1024)} %get-tuple-element.392), kind=kLoop, calls=%fused_computation.43.clone.1 | loop fusion | flops 29884416 | bytes 8388632 | tf_op jit(solution)/shard_map/sin | solution.py:35
  247.5 2.7 copy.88
  250.2 5.8 %copy.89 = f32[3,8,64,512]{2,3,1,0:T(8,128)} copy(f32[3,8,64,512]{3,2,1,0:T(8,128)} %bitcast.89) | data formatting | bytes 6291456 | tf_op jit(solution)/shard_map/reshape.31
  255.9 4.8 %copy.90 = f32[1,3,512,512]{3,2,1,0:T(8,128)} copy(f32[1,3,512,512]{3,1,2,0:T(4,128)} %bitcast.87) | data formatting | bytes 6291456 | tf_op jit(solution)/shard_map/while
  260.8 5.8 %copy.91 = f32[3,8,64,512]{2,3,1,0:T(8,128)} copy(f32[3,8,64,512]{3,2,1,0:T(8,128)} %bitcast.90) | data formatting | bytes 6291456 | tf_op jit(solution)/shard_map/reshape.26
  266.5 4.9 %copy.92 = f32[1,3,512,512]{3,2,1,0:T(8,128)} copy(f32[1,3,512,512]{3,1,2,0:T(4,128)} %bitcast.93) | data formatting | bytes 6291456 | tf_op jit(solution)/shard_map/while
  271.4 5.8 %copy.93 = f32[3,8,64,512]{2,3,1,0:T(8,128)} copy(f32[3,8,64,512]{3,2,1,0:T(8,128)} %bitcast.91) | data formatting | bytes 6291456 | tf_op jit(solution)/shard_map/reshape.23
  277.2 4.8 %copy.95 = f32[1,3,512,512]{3,2,1,0:T(8,128)} copy(f32[1,3,512,512]{3,1,2,0:T(4,128)} %bitcast.94) | data formatting | bytes 6291456 | tf_op jit(solution)/shard_map/while
  282.0 5.8 %copy.96 = f32[3,8,64,512]{2,3,1,0:T(8,128)} copy(f32[3,8,64,512]{3,2,1,0:T(8,128)} %bitcast.92) | data formatting | bytes 6291456 | tf_op jit(solution)/shard_map/reshape.20
  287.8 10.7 %select_convert_fusion.3 = (bf16[3,8,64,512]{2,3,1,0:T(8,128)(2,1)S(1)}, bf16[3,8,64,512]{2,3,1,0:T(8,128)(2,1)S(1)}) fusion(f32[3,8,64,512]{2,3,1,0:T(8,128)} %copy.89, f32[3,8,64,512]{2,3,1,0:T(8,128)} %copy.91, pred[8,64,512]{1,2,0:T(8,128)(4,1)S(1)} %add_compare_fusion.2, f32[3,8,64,512]{2,3,1,0:T(8,128)} %copy.93, f32[8,64,512]{1,2,0:T(8,128)S(1)} %copy.94, ...), kind=kLoop, calls=%fused_computation.22.clone.1 | loop fusion | flops 12582912 | bytes 18087936 | tf_op jit(solution)/shard_map/convert.4
  298.5 3.6 fusion.85
  302.1 4.1 fusion.86
  307.8 3.9 multiply_reduce_fusion.2
  312.6 1.6 select_reduce_fusion.2
  316.3 16.6 %fusion.84 = (f32[262144]{0:T(1024)}, f32[262144]{0:T(1024)S(1)}, f32[1,1,262144]{2,1,0:T(1,128)}) fusion(bf16[2,2,262144]{2,1,0:T(2,128)(2,1)} %get-tuple-element.387, s32[]{:T(128)} %get-tuple-element.363, s32[]{:T(128)S(6)} %add.959), kind=kLoop, calls=%fused_computation.62.clone.1 | loop fusion | flops 1310720 | bytes 4194312 | tf_op jit(solution)/shard_map/while/body/eval_jaxpr/convert_element_type | solution.py:79
  333.8 1.4 reshape.324
  335.2 1.9 copy.97
  338.7 42.2 %fusion.83 = (f32[3,262144]{1,0:T(4,128)S(1)}, f32[3,262144]{1,0:T(4,128)}) fusion(s32[3]{0:T(128)S(1)} %get-tuple-element.393, s32[262144]{0:T(1024)} %get-tuple-element.394, s32[3]{0:T(128)S(1)} %get-tuple-element.391, s32[262144]{0:T(1024)} %get-tuple-element.392), kind=kLoop, calls=%fused_computation.43.clone.1 | loop fusion | flops 29884416 | bytes 8388632 | tf_op jit(solution)/shard_map/sin | solution.py:35
  380.9 2.7 copy.88
  383.6 5.8 %copy.89 = f32[3,8,64,512]{2,3,1,0:T(8,128)} copy(f32[3,8,64,512]{3,2,1,0:T(8,128)} %bitcast.89) | data formatting | bytes 6291456 | tf_op jit(solution)/shard_map/reshape.31
  389.4 4.8 %copy.90 = f32[1,3,512,512]{3,2,1,0:T(8,128)} copy(f32[1,3,512,512]{3,1,2,0:T(4,128)} %bitcast.87) | data formatting | bytes 6291456 | tf_op jit(solution)/shard_map/while
  394.2 5.8 %copy.91 = f32[3,8,64,512]{2,3,1,0:T(8,128)} copy(f32[3,8,64,512]{3,2,1,0:T(8,128)} %bitcast.90) | data formatting | bytes 6291456 | tf_op jit(solution)/shard_map/reshape.26
  400.0 4.9 %copy.92 = f32[1,3,512,512]{3,2,1,0:T(8,128)} copy(f32[1,3,512,512]{3,1,2,0:T(4,128)} %bitcast.93) | data formatting | bytes 6291456 | tf_op jit(solution)/shard_map/while
  404.9 5.8 %copy.93 = f32[3,8,64,512]{2,3,1,0:T(8,128)} copy(f32[3,8,64,512]{3,2,1,0:T(8,128)} %bitcast.91) | data formatting | bytes 6291456 | tf_op jit(solution)/shard_map/reshape.23
  410.6 4.8 %copy.95 = f32[1,3,512,512]{3,2,1,0:T(8,128)} copy(f32[1,3,512,512]{3,1,2,0:T(4,128)} %bitcast.94) | data formatting | bytes 6291456 | tf_op jit(solution)/shard_map/while
  415.5 5.8 %copy.96 = f32[3,8,64,512]{2,3,1,0:T(8,128)} copy(f32[3,8,64,512]{3,2,1,0:T(8,128)} %bitcast.92) | data formatting | bytes 6291456 | tf_op jit(solution)/shard_map/reshape.20
  421.2 10.7 %select_convert_fusion.3 = (bf16[3,8,64,512]{2,3,1,0:T(8,128)(2,1)S(1)}, bf16[3,8,64,512]{2,3,1,0:T(8,128)(2,1)S(1)}) fusion(f32[3,8,64,512]{2,3,1,0:T(8,128)} %copy.89, f32[3,8,64,512]{2,3,1,0:T(8,128)} %copy.91, pred[8,64,512]{1,2,0:T(8,128)(4,1)S(1)} %add_compare_fusion.2, f32[3,8,64,512]{2,3,1,0:T(8,128)} %copy.93, f32[8,64,512]{1,2,0:T(8,128)S(1)} %copy.94, ...), kind=kLoop, calls=%fused_computation.22.clone.1 | loop fusion | flops 12582912 | bytes 18087936 | tf_op jit(solution)/shard_map/convert.4
  432.0 3.6 fusion.85
  435.6 4.1 fusion.86
  441.3 3.9 multiply_reduce_fusion.2
  446.1 1.6 select_reduce_fusion.2
  (62 shorter events, 14.0 us)
Async XLA Ops:
  7.2 12.7 %copy-start = (bf16[32,2,16384]{2,1,0:T(2,128)(2,1)S(1)}, bf16[32,2,16384]{2,1,0:T(2,128)(2,1)}, u32[]{:S(2)}) copy-start(bf16[32,2,16384]{2,1,0:T(2,128)(2,1)} %param.9) | copy-start | bytes 6291460
  7.2 165.2 %all-reduce.2.cloned.1.call-start = ((), (), s32[]{:S(2)}) async-start(), calls=%async_computation.1 | async-start | bytes 8388608 | tf_op jit(solution)/shard_map/psum | solution.py:16
  18.3 0.7 copy-start.7
  26.0 9.4 %copy-start.2 = (s32[32]{0:T(128)S(1)}, s32[32]{0:T(128)}, u32[]{:S(2)}) copy-start(s32[32]{0:T(128)} %param.10) | copy-start | bytes 388
  26.0 151.3 %all-to-all-start = ((bf16[16,2,2,16384]{3,2,1,0:T(2,128)(2,1)}), bf16[16,2,2,16384]{3,2,1,0:T(2,128)(2,1)}, u32[]{:S(2)}, u32[]{:S(2)}) async-start(bf16[16,2,2,16384]{3,2,1,0:T(2,128)(2,1)} %bitcast.96), calls=%async_computation | async-start | bytes 4194304 | tf_op jit(solution)/shard_map/all_to_all | solution.py:52
  55.6 1.6 copy-start.6
  287.8 10.7 %copy-start.5 = (bf16[8,1024,128]{2,1,0:T(8,128)(2,1)S(1)}, bf16[8,1024,128]{2,1,0:T(8,128)(2,1)}, u32[]{:S(2)}) copy-start(bf16[8,1024,128]{2,1,0:T(8,128)(2,1)} %get-tuple-element.389) | copy-start | bytes 6291460 | tf_op jit(solution)/shard_map/while
  306.2 1.6 copy-start.4
  307.8 4.8 %copy-start.3 = (f32[1,1,262144]{2,1,0:T(1,128)S(1)}, f32[1,1,262144]{2,1,0:T(1,128)}, u32[]{:S(2)}) copy-start(f32[1,1,262144]{2,1,0:T(1,128)} %get-tuple-element.343) | copy-start | bytes 3145732 | tf_op jit(solution)/shard_map/while
  421.2 10.7 %copy-start.5 = (bf16[8,1024,128]{2,1,0:T(8,128)(2,1)S(1)}, bf16[8,1024,128]{2,1,0:T(8,128)(2,1)}, u32[]{:S(2)}) copy-start(bf16[8,1024,128]{2,1,0:T(8,128)(2,1)} %get-tuple-element.389) | copy-start | bytes 6291460 | tf_op jit(solution)/shard_map/while
  439.7 1.6 copy-start.4
  441.3 4.8 %copy-start.3 = (f32[1,1,262144]{2,1,0:T(1,128)S(1)}, f32[1,1,262144]{2,1,0:T(1,128)}, u32[]{:S(2)}) copy-start(f32[1,1,262144]{2,1,0:T(1,128)} %get-tuple-element.343) | copy-start | bytes 3145732 | tf_op jit(solution)/shard_map/while
  449.8 0.5 copy-start.8
  449.8 0.5 copy-start.9
  449.8 1.6 copy-start.1
Sparse Core Ops, SparseCore 0:
  18.5 153.8 all-reduce.1
where the time goes:
time: 464 us; the launch traced here: 458 us
  other arithmetic  195 us (42%)
  waiting for transfers between devices  115 us (25%)
  local copies, waits for them, and re-layouts  106 us (23%)
  matrix products  15.1 us (3%)
  between operations  15.1 us (3%)
  starting transfers between devices  7.82 us (2%)
    psum x1, waiting for transfers between devices, spread(): return lax.psum(block, axis)  115 us
    sin x2, other arithmetic, slide_phases(): return (jnp.cos(angles), jnp.sin(angles))  84.5 us
    another operation x8, local copies, waits for them, and re-layouts  46.1 us
    another operation x9, other arithmetic  40.9 us
    while x20, local copies, waits for them, and re-layouts  35.1 us
    convert_element_type x2, other arithmetic, filter_one(): wave_re = waveform[0].astype(jnp.float32)  33.1 us
    select_n x1, other arithmetic, spread(): jnp.where(lax.axis_index(axis) == owner, block, jnp.zeros_like(block))  10.3 us
  transfers between devices with their start and end apart: 2, of which 1 were waited for; matrix products, arithmetic and copies ran while one was open for 8% of the time, Pallas kernels for 0%

commit v1 on v0

--- a/solution.py
+++ b/solution.py
@@ -2,6 +2,7 @@
 import jax.numpy as jnp
 from jax import lax
 from jax.sharding import PartitionSpec as P
+from jax.lax import all_gather
 
 DET = 3
 ROWS = 512
@@ -13,7 +14,12 @@
 
 def spread(block, axis, owner):
     block = jnp.where(lax.axis_index(axis) == owner, block, jnp.zeros_like(block))
-    return lax.psum(block, axis)
+
+    def axis_part_scan(mine):
+        prior = all_gather(mine, axis_name=axis)
+        return jnp.sum(prior, axis=0)
+
+    return axis_part_scan(block)
 
 
 def turn_table(left_ids, right_ids, period):

time: 464 us -> 662 us (1.43)
  the two profiles are of different devices: /device:TPU:0 before, /device:TPU:9 now
where the time goes in v1:
time: 662 us; the launch traced here: 658 us
  waiting for transfers between devices  251 us (38%)
  other arithmetic  240 us (36%)
  local copies, waits for them, and re-layouts  114 us (17%)
  loops' own time  16.1 us (2%)
  matrix products  15.1 us (2%)
  between operations  15.1 us (2%)
  starting transfers between devices  6.94 us (1%)
    all_gather x1, waiting for transfers between devices, axis_part_scan(): prior = all_gather(mine, axis_name=axis)  204 us
    sin x2, other arithmetic, slide_phases(): return (jnp.cos(angles), jnp.sin(angles))  84.5 us
    reduce_sum x1, other arithmetic, axis_part_scan(): return jnp.sum(prior, axis=0)  48.8 us
    all_to_all x1, waiting for transfers between devices, body(): lax.all_to_all(picked, 'tpl', split_axis=0, concat_axis=3, tiled=True)[0]  46.6 us
    another operation x8, local copies, waits for them, and re-layouts  46.1 us
    another operation x9, other arithmetic  40.9 us
    while x20, local copies, waits for them, and re-layouts  35.1 us
    convert_element_type x2, other arithmetic, filter_one(): wave_re = waveform[0].astype(jnp.float32)  33.1 us
  transfers between devices with their start and end apart: 2, of which 2 were waited for; matrix products, arithmetic and copies ran while one was open for 5% of the time, Pallas kernels for 0%

profile of v1, /device:TPU:9, one launch (start us, length us, event | category | flops | bytes accessed | tf_op | source)
XLA Modules:
  0.0 657.6 jit_solution(1576149197317656751)
XLA Ops:
  8.0 4.2 broadcast_select_fusion
  13.8 6.2 gather_fusion.2
  19.9 6.9 %all-to-all-start = ((bf16[16,2,2,16384]{3,2,1,0:T(2,128)(2,1)}), bf16[16,2,2,16384]{3,2,1,0:T(2,128)(2,1)}, u32[]{:S(2)}, u32[]{:S(2)}) async-start(bf16[16,2,2,16384]{3,2,1,0:T(2,128)(2,1)} %bitcast.88), calls=%async_computation | async-start | bytes 4194304 | tf_op jit(solution)/shard_map/all_to_all | solution.py:58
  27.0 4.0 fusion.63
  30.9 4.3 negate_convert_fusion.1
  35.3 8.7 %negate_convert_fusion = (bf16[8,512,64]{2,1,0:T(8,128)(2,1)S(1)}, bf16[8,512,64]{2,1,0:T(8,128)(2,1)S(1)}, bf16[8,512,64]{2,1,0:T(8,128)(2,1)S(1)}) fusion(s32[8,64]{1,0:T(8,128)S(1)} %multiply_add_fusion.2), kind=kLoop, calls=%fused_computation.81 | loop fusion | flops 4718592 | bytes 1574912 | tf_op jit(solution)/shard_map/convert.20
  44.0 2.5 maximum_maximum_fusion
  46.5 1.6 maximum_maximum_fusion.1
  50.2 46.6 %all-to-all-done = bf16[16,2,2,16384]{3,2,1,0:T(2,128)(2,1)} async-done(((bf16[16,2,2,16384]{3,2,1,0:T(2,128)(2,1)}), bf16[16,2,2,16384]{3,2,1,0:T(2,128)(2,1)}, u32[]{:S(2)}, u32[]{:S(2)}) %all-to-all-start) | async-done | bytes 2097184 | tf_op jit(solution)/shard_map/all_to_all | solution.py:58
  96.8 2.7 copy.63
  99.5 2.5 squeeze.23
  102.1 204.0 %all-gather.2.cloned.1.call-done = bf16[16,3,2,262144]{3,2,1,0:T(2,128)(2,1)} async-done(((bf16[1,3,2,262144]{3,2,1,0:T(2,128)(2,1)}), bf16[16,3,2,262144]{3,2,1,0:T(2,128)(2,1)}) %all-gather.2.cloned.1.call-update) | async-done | bytes 50331664 | tf_op jit(solution)/shard_map/all_gather | solution.py:19
  306.1 48.8 %reduce_sum.30 = bf16[3,2,262144]{2,1,0:T(2,128)(2,1)} reduce(bf16[16,3,2,262144]{3,2,1,0:T(2,128)(2,1)} %all-gather.2.cloned.1.call-done, bf16[]{:T(256)} %constant.126.clone.1), dimensions={0}, to_apply=%region_0.1 | reduce | flops 23592960 | bytes 53477376 | tf_op jit(solution)/shard_map/reduce_sum | solution.py:20
  354.8 7.9 %slice_convert_fusion = (f32[3,1,262144]{2,1,0:T(1,128)S(1)}, f32[3,1,262144]{2,1,0:T(1,128)S(1)}) fusion(bf16[3,2,262144]{2,1,0:T(2,128)(2,1)} %reduce_sum.30), kind=kLoop, calls=%fused_computation.71 | loop fusion | flops 1572864 | bytes 9437184 | tf_op jit(solution)/shard_map/convert_element_type | solution.py:80
  362.7 7.5 %copy_bitcast_fusion = (f32[3,262144]{1,0:T(4,128)}, f32[3,262144]{1,0:T(4,128)}) fusion(f32[3,1,262144]{2,1,0:T(1,128)S(1)} %get-tuple-element.234, f32[3,1,262144]{2,1,0:T(1,128)S(1)} %get-tuple-element.235), kind=kLoop, calls=%fused_computation.69 | loop fusion | bytes 12582912
  370.2 278.8 %while.15 = (s32[]{:T(128)}, f32[2]{0:T(128)S(1)}, f32[2]{0:T(128)S(1)}, s32[2]{0:T(128)S(1)}, f32[3,262144]{1,0:T(4,128)}, /*index=5*/bf16[2,2,262144]{2,1,0:T(...) while((s32[]{:T(128)}, f32[2]{0:T(128)S(1)}, ...), condition=%wide.region_5.6_spmd.clone.clone.clone, body=%wide.region_1.5_spmd.clone.clone.clone.sunk | while | flops 6514016256 | bytes 146276784 | solution.py:116
  382.6 16.5 %fusion.81 = (f32[262144]{0:T(1024)}, f32[262144]{0:T(1024)S(1)}, f32[1,1,262144]{2,1,0:T(1,128)}) fusion(bf16[2,2,262144]{2,1,0:T(2,128)(2,1)} %get-tuple-element.389, s32[]{:T(128)} %get-tuple-element.365, s32[]{:T(128)S(6)} %add.957), kind=kLoop, calls=%fused_computation.62.clone.1 | loop fusion | flops 1310720 | bytes 4194312 | tf_op jit(solution)/shard_map/while/body/eval_jaxpr/convert_element_type | solution.py:85
  401.3 2.0 copy.93
  404.9 42.3 %fusion.80 = (f32[3,262144]{1,0:T(4,128)S(1)}, f32[3,262144]{1,0:T(4,128)}) fusion(s32[3]{0:T(128)S(1)} %get-tuple-element.395, s32[262144]{0:T(1024)} %get-tuple-element.396, s32[3]{0:T(128)S(1)} %get-tuple-element.393, s32[262144]{0:T(1024)} %get-tuple-element.394), kind=kLoop, calls=%fused_computation.43.clone.1 | loop fusion | flops 29884416 | bytes 8388632 | tf_op jit(solution)/shard_map/sin | solution.py:41
  447.1 2.7 copy.84
  449.9 5.7 copy.85
  455.6 4.8 copy.86
  460.4 5.8 copy.87
  466.2 4.9 copy.88
  471.1 5.8 copy.89
  476.8 4.8 copy.91
  481.7 5.8 copy.92
  487.4 10.7 %select_convert_fusion.3 = (bf16[3,8,64,512]{2,3,1,0:T(8,128)(2,1)S(1)}, bf16[3,8,64,512]{2,3,1,0:T(8,128)(2,1)S(1)}) fusion(f32[3,8,64,512]{2,3,1,0:T(8,128)} %copy.85, f32[3,8,64,512]{2,3,1,0:T(8,128)} %copy.87, pred[8,64,512]{1,2,0:T(8,128)(4,1)S(1)} %add_compare_fusion.2, f32[3,8,64,512]{2,3,1,0:T(8,128)} %copy.89, f32[8,64,512]{1,2,0:T(8,128)S(1)} %copy.90, ...), kind=kLoop, calls=%fused_computation.22.clone.1 | loop fusion | flops 12582912 | bytes 18087936 | tf_op jit(solution)/shard_map/convert.5
  498.1 3.6 fusion.82
  501.8 4.1 fusion.83
  507.5 3.9 multiply_reduce_fusion.2
  512.3 1.5 select_reduce_fusion.2
  515.8 16.6 %fusion.81 = (f32[262144]{0:T(1024)}, f32[262144]{0:T(1024)S(1)}, f32[1,1,262144]{2,1,0:T(1,128)}) fusion(bf16[2,2,262144]{2,1,0:T(2,128)(2,1)} %get-tuple-element.389, s32[]{:T(128)} %get-tuple-element.365, s32[]{:T(128)S(6)} %add.957), kind=kLoop, calls=%fused_computation.62.clone.1 | loop fusion | flops 1310720 | bytes 4194312 | tf_op jit(solution)/shard_map/while/body/eval_jaxpr/convert_element_type | solution.py:85
  534.5 2.0 copy.93
  538.1 42.3 %fusion.80 = (f32[3,262144]{1,0:T(4,128)S(1)}, f32[3,262144]{1,0:T(4,128)}) fusion(s32[3]{0:T(128)S(1)} %get-tuple-element.395, s32[262144]{0:T(1024)} %get-tuple-element.396, s32[3]{0:T(128)S(1)} %get-tuple-element.393, s32[262144]{0:T(1024)} %get-tuple-element.394), kind=kLoop, calls=%fused_computation.43.clone.1 | loop fusion | flops 29884416 | bytes 8388632 | tf_op jit(solution)/shard_map/sin | solution.py:41
  580.4 2.7 copy.84
  583.1 5.7 copy.85
  588.8 4.8 copy.86
  593.6 5.8 copy.87
  599.4 4.9 copy.88
  604.3 5.8 copy.89
  610.0 4.8 copy.91
  614.9 5.8 copy.92
  620.7 10.7 %select_convert_fusion.3 = (bf16[3,8,64,512]{2,3,1,0:T(8,128)(2,1)S(1)}, bf16[3,8,64,512]{2,3,1,0:T(8,128)(2,1)S(1)}) fusion(f32[3,8,64,512]{2,3,1,0:T(8,128)} %copy.85, f32[3,8,64,512]{2,3,1,0:T(8,128)} %copy.87, pred[8,64,512]{1,2,0:T(8,128)(4,1)S(1)} %add_compare_fusion.2, f32[3,8,64,512]{2,3,1,0:T(8,128)} %copy.89, f32[8,64,512]{1,2,0:T(8,128)S(1)} %copy.90, ...), kind=kLoop, calls=%fused_computation.22.clone.1 | loop fusion | flops 12582912 | bytes 18087936 | tf_op jit(solution)/shard_map/convert.5
  631.4 3.6 fusion.82
  635.0 4.1 fusion.83
  640.7 3.9 multiply_reduce_fusion.2
  645.5 1.5 select_reduce_fusion.2
  (64 shorter events, 18.4 us)
Async XLA Ops:
  7.2 6.6 %copy-start = (bf16[32,2,16384]{2,1,0:T(2,128)(2,1)S(1)}, bf16[32,2,16384]{2,1,0:T(2,128)(2,1)}, u32[]{:S(2)}) copy-start(bf16[32,2,16384]{2,1,0:T(2,128)(2,1)} %param.9) | copy-start | bytes 6291460
  7.2 298.9 %all-gather.2.cloned.1.call-start = ((), (), s32[]{:S(2)}) async-start(), calls=%async_computation.1 | async-start | bytes 53477376 | tf_op jit(solution)/shard_map/all_gather | solution.py:19
  12.2 0.7 copy-start.7
  19.9 76.9 %all-to-all-start = ((bf16[16,2,2,16384]{3,2,1,0:T(2,128)(2,1)}), bf16[16,2,2,16384]{3,2,1,0:T(2,128)(2,1)}, u32[]{:S(2)}, u32[]{:S(2)}) async-start(bf16[16,2,2,16384]{3,2,1,0:T(2,128)(2,1)} %bitcast.88), calls=%async_computation | async-start | bytes 4194304 | tf_op jit(solution)/shard_map/all_to_all | solution.py:58
  46.5 1.6 copy-start.2
  46.5 2.2 copy-start.6
  487.4 10.7 %copy-start.5 = (bf16[8,1024,128]{2,1,0:T(8,128)(2,1)S(1)}, bf16[8,1024,128]{2,1,0:T(8,128)(2,1)}, u32[]{:S(2)}) copy-start(bf16[8,1024,128]{2,1,0:T(8,128)(2,1)} %get-tuple-element.391) | copy-start | bytes 6291460 | tf_op jit(solution)/shard_map/while
  505.9 1.6 copy-start.4
  507.5 4.9 copy-start.3
  620.6 10.7 %copy-start.5 = (bf16[8,1024,128]{2,1,0:T(8,128)(2,1)S(1)}, bf16[8,1024,128]{2,1,0:T(8,128)(2,1)}, u32[]{:S(2)}) copy-start(bf16[8,1024,128]{2,1,0:T(8,128)(2,1)} %get-tuple-element.391) | copy-start | bytes 6291460 | tf_op jit(solution)/shard_map/while
  639.1 1.6 copy-start.4
  640.7 4.9 copy-start.3
  649.0 0.5 copy-start.8
  649.0 0.5 copy-start.9
  649.0 1.6 copy-start.1
Sparse Core Ops, SparseCore 0:
  12.3 293.6 all-gather.1
